TPU v7x, 32 devices: a whole 2x2x4 slice. The times are simulated.
32 devices in a mesh: groups: 2 (over y), expert: 4 (over z), tensor: 4 (over x, core), sub: 1.
Axes of the slice: x: 2, y: 2, z: 4, core: 2. Of those that a mesh axis runs over, the one named last changes fastest.
Arguments:
- hidden_rows: bfloat16 [4, 320, 4096], P(None, ('groups', 'expert', 'tensor')), parts along dimension 1, may hold values from -6 to 6
- expert_ids: int32 [4, 320, 8], P(None, ('groups', 'expert', 'tensor')), parts along dimension 1, may hold values from 0 to 15, all different within a row; in each aligned block of 10 rows (0 to 9, 10 to 19, ..., all dimensions but the last counted through in order) at most 5 rows name the same one
- accepted: int32 [4, 64], P(None, ('groups', 'expert', 'tensor')), parts along dimension 1, may hold values from 0 to 4
- norm_gain: float32 [4096], replicated, may hold values from 0.5 to 1.5
- router: bfloat16 [4096, 16], replicated, may hold values from -0.0625 to 0.0625
- gate_weight: bfloat16 [16, 4096, 768], P(('expert', 'tensor'), None, 'sub'), may hold values from -0.09375 to 0.09375
- up_weight: bfloat16 [16, 4096, 768], P(('expert', 'tensor'), None, 'sub'), may hold values from -0.09375 to 0.09375
- down_weight: bfloat16 [16, 768, 4096], P(('expert', 'tensor'), 'sub'), may hold values from -0.21875 to 0.21875
- draft_gain: float32 [4096], replicated, may hold values from 0.5 to 1.5
- draft_gate: bfloat16 [4096, 6144], P(None, ('expert', 'tensor')), may hold values from -0.09375 to 0.09375
- draft_up: bfloat16 [4096, 6144], P(None, ('expert', 'tensor')), may hold values from -0.09375 to 0.09375
- draft_down: bfloat16 [6144, 4096], P(('expert', 'tensor')), may hold values from -0.078125 to 0.078125
- final_gain: float32 [4096], replicated, may hold values from 0.5 to 1.5
Outputs:
- verified: bfloat16 [4, 320, 4096], P(None, ('groups', 'expert', 'tensor')), parts along dimension 1
- draft_out: bfloat16 [4, 64, 4096], P(None, ('groups', 'expert', 'tensor')), parts along dimension 1
There are 2 independent parts, one for each index of `groups`. A program takes and returns all parts, laid end to end along the dimension named above; an argument that names none is the same for every part. Nothing has to cross between parts.
Inputs may be any that keep to these rules, and one draw needn't show every extreme that they name: `expert_ids`: the 8 ids of a row differ. In each aligned block of 10 rows no expert is named by more than 5 rows, and in some block one expert is named by exactly 5 rows.
All inputs are finite; a program needn't handle non-finite values.
Results may differ from a plain program's by a relative error of at most 0.0068.
Values may be sent and summed in bfloat16 or wider, within the bound.
A program may use at most 128 MiB of HBM per device.

v0:
```python
import jax
import jax.numpy as jnp
from jax import lax
from jax.sharding import PartitionSpec as P

EPSILON = 1e-06


def rms_scale(values, weights):
    values = values.astype(jnp.float32)
    mean_square = jnp.mean(values * values, axis=-1, keepdims=True)
    return values * lax.rsqrt(mean_square + EPSILON) * weights


def local(
    hidden_rows,
    expert_ids,
    accepted,
    norm_gain,
    router,
    gate_weight,
    up_weight,
    down_weight,
    draft_gain,
    draft_gate,
    draft_up,
    draft_down,
    final_gain,
):
    rounds_total = hidden_rows.shape[0]
    rows_here = hidden_rows.shape[1]
    feature_width = hidden_rows.shape[2]
    top_count = expert_ids.shape[2]
    expert_count = router.shape[1]
    requests_here = accepted.shape[1]
    draft_rows = rows_here // requests_here
    capacity = max(2, (rows_here * top_count + expert_count - 1) // expert_count)
    expert_range = jnp.arange(expert_count, dtype=jnp.int32)
    slot_range = jnp.arange(capacity, dtype=jnp.float32)
    highest = lax.Precision.HIGHEST
    verified_list = []
    draft_list = []
    for round_index in range(rounds_total):
        rows = hidden_rows[round_index]
        chosen_ids = expert_ids[round_index]
        normed = rms_scale(rows, norm_gain).astype(jnp.bfloat16)
        logits = jnp.dot(normed, router, preferred_element_type=jnp.float32)
        expert_hot = (chosen_ids[:, :, None] == expert_range[None, None, :]).astype(jnp.float32)
        chosen = jnp.sum(expert_hot * logits[:, None, :], axis=2)
        exp_values = jnp.exp(chosen)
        gate_share = exp_values / jnp.sum(exp_values, axis=1, keepdims=True)
        flat_hot = expert_hot.reshape(rows_here * top_count, expert_count)
        rank_values = jnp.cumsum(flat_hot, axis=0) - 1.0
        positions = jnp.sum(rank_values * flat_hot, axis=1).reshape(rows_here, top_count)
        slot_hot = (positions[:, :, None] == slot_range[None, None, :]).astype(jnp.float32)
        send_table = jnp.einsum("rke,rkc->ecr", expert_hot, slot_hot)
        gate_table = jnp.einsum(
            "rke,rkc->ecr", expert_hot * gate_share[:, :, None], slot_hot, precision=highest
        )
        outgoing = jnp.einsum(
            "ecr,rd->ecd",
            send_table.astype(jnp.bfloat16),
            normed,
            preferred_element_type=jnp.float32,
        ).astype(jnp.bfloat16)
        received = lax.all_to_all(
            outgoing, ("expert", "tensor"), split_axis=0, concat_axis=0, tiled=True
        )
        sources = received.shape[0]
        item_count = received.shape[1]
        flat_rows = received.reshape(sources * item_count, feature_width)
        gate_values = jnp.dot(flat_rows, gate_weight[0], preferred_element_type=jnp.float32)
        up_values = jnp.dot(flat_rows, up_weight[0], preferred_element_type=jnp.float32)
        active = (jax.nn.silu(gate_values) * up_values).astype(jnp.bfloat16)
        partial_out = jnp.dot(active, down_weight[0], preferred_element_type=jnp.float32)
        partial_out = partial_out.reshape(sources, item_count, feature_width)
        processed = lax.psum(partial_out.astype(jnp.bfloat16), "sub")
        returned = lax.all_to_all(
            processed, ("expert", "tensor"), split_axis=0, concat_axis=0, tiled=True
        )
        mixed_rows = rows.astype(jnp.float32) + jnp.einsum(
            "ecr,ecd->rd", gate_table, returned.astype(jnp.float32), precision=highest
        )
        verified = mixed_rows.astype(jnp.bfloat16)
        wanted = jnp.arange(requests_here, dtype=jnp.int32) * draft_rows + accepted[round_index]
        select_table = (jnp.arange(rows_here, dtype=jnp.int32)[None, :] == wanted[:, None]).astype(
            jnp.bfloat16
        )
        features = jnp.dot(select_table, verified, preferred_element_type=jnp.float32).astype(
            jnp.bfloat16
        )
        draft_input = rms_scale(features, draft_gain).astype(jnp.bfloat16)
        piece_rows = lax.all_gather(draft_input, ("expert", "tensor"), axis=0, tiled=True)
        gate_part = jnp.dot(piece_rows, draft_gate, preferred_element_type=jnp.float32)
        up_part = jnp.dot(piece_rows, draft_up, preferred_element_type=jnp.float32)
        unit_rows = (jax.nn.silu(gate_part) * up_part).astype(jnp.bfloat16)
        summed = lax.psum_scatter(
            jnp.dot(unit_rows, draft_down, preferred_element_type=jnp.float32),
            ("expert", "tensor"),
            scatter_dimension=0,
            tiled=True,
        )
        draft_out = rms_scale(features.astype(jnp.float32) + summed, final_gain).astype(
            jnp.bfloat16
        )
        verified_list.append(verified)
        draft_list.append(draft_out)
    return (jnp.stack(verified_list, axis=0), jnp.stack(draft_list, axis=0))


def solution(mesh):
    placed = (
        P(None, ("groups", "expert", "tensor"), None),
        P(None, ("groups", "expert", "tensor"), None),
        P(None, ("groups", "expert", "tensor")),
        P(),
        P(),
        P(("expert", "tensor"), None, "sub"),
        P(("expert", "tensor"), None, "sub"),
        P(("expert", "tensor"), "sub", None),
        P(),
        P(None, ("expert", "tensor")),
        P(None, ("expert", "tensor")),
        P(("expert", "tensor"), None),
        P(),
    )
    return jax.shard_map(
        local,
        mesh=mesh,
        in_specs=placed,
        out_specs=(
            P(None, ("groups", "expert", "tensor"), None),
            P(None, ("groups", "expert", "tensor"), None),
        ),
        check_vma=False,
    )
```

profile of v0, /device:TPU:0, one launch (start us, length us, event | category | flops | bytes accessed | tf_op | source)
XLA Modules:
  0.0 499.1 jit_solution(5771111974080170452)
XLA Ops:
  7.2 1.5 fusion.217
  9.4 2.9 fusion.216
  15.2 7.4 %all-to-all-start.6 = ((bf16[16,5,4096]{2,1,0:T(8,128)(2,1)}), bf16[16,5,4096]{2,1,0:T(8,128)(2,1)}, u32[]{:S(2)}, u32[]{:S(2)}) async-start(bf16[16,5,4096]{2,1,0:T(8,128)(2,1)} %copy.76), calls=%async_computation.6 | async-start | bytes 2097152 | tf_op jit(solution)/shard_map/all_to_all | solution.py:66
  38.1 1.4 select_reduce_fusion.5
  54.7 1.4 copy.49
  56.1 1.6 slice_reduce_fusion.3
  60.6 6.0 %all-to-all-start.4 = ((bf16[16,5,4096]{2,1,0:T(8,128)(2,1)}), bf16[16,5,4096]{2,1,0:T(8,128)(2,1)}, u32[]{:S(2)}, u32[]{:S(2)}) async-start(bf16[16,5,4096]{2,1,0:T(8,128)(2,1)} %copy.67), calls=%async_computation.4 | async-start | bytes 2097152 | tf_op jit(solution)/shard_map/all_to_all | solution.py:66
  71.3 18.3 %all-to-all-done.4 = bf16[16,5,4096]{2,1,0:T(8,128)(2,1)} async-done(((bf16[16,5,4096]{2,1,0:T(8,128)(2,1)}), bf16[16,5,4096]{2,1,0:T(8,128)(2,1)}, u32[]{:S(2)}, u32[]{:S(2)}) %all-to-all-start.4) | async-done | bytes 655392 | tf_op jit(solution)/shard_map/all_to_all | solution.py:66
  89.6 6.8 %all-to-all-start = ((bf16[16,5,4096]{2,1,0:T(8,128)(2,1)}), bf16[16,5,4096]{2,1,0:T(8,128)(2,1)}, u32[]{:S(2)}, u32[]{:S(2)}) async-start(bf16[16,5,4096]{2,1,0:T(8,128)(2,1)} %copy.49), calls=%async_computation | async-start | bytes 2097152 | tf_op jit(solution)/shard_map/all_to_all | solution.py:66
  96.6 1.6 convolution_bitcast_fusion.4
  98.2 1.5 convolution_bitcast_fusion.5
  99.8 1.5 convolution_bitcast_fusion.6
  102.2 2.3 reshape.263
  104.5 14.9 %all-to-all-done = bf16[16,5,4096]{2,1,0:T(8,128)(2,1)} async-done(((bf16[16,5,4096]{2,1,0:T(8,128)(2,1)}), bf16[16,5,4096]{2,1,0:T(8,128)(2,1)}, u32[]{:S(2)}, u32[]{:S(2)}) %all-to-all-start) | async-done | bytes 655392 | tf_op jit(solution)/shard_map/all_to_all | solution.py:66
  119.4 6.8 %all-to-all-start.2 = ((bf16[16,5,4096]{2,1,0:T(8,128)(2,1)}), bf16[16,5,4096]{2,1,0:T(8,128)(2,1)}, u32[]{:S(2)}, u32[]{:S(2)}) async-start(bf16[16,5,4096]{2,1,0:T(8,128)(2,1)} %copy.58), calls=%async_computation.2 | async-start | bytes 2097152 | tf_op jit(solution)/shard_map/all_to_all | solution.py:66
  126.2 4.2 fusion.18
  130.5 4.7 fusion.63
  135.1 1.6 dot_general.176
  136.8 4.1 fusion.30
  140.9 1.4 copy.69
  142.3 2.4 reshape.261
  144.6 4.5 all-to-all-done.2
  149.2 6.9 %all-to-all-start.5 = ((bf16[16,5,4096]{2,1,0:T(8,128)(2,1)}), bf16[16,5,4096]{2,1,0:T(8,128)(2,1)}, u32[]{:S(2)}, u32[]{:S(2)}) async-start(bf16[16,5,4096]{2,1,0:T(8,128)(2,1)} %copy.69), calls=%async_computation.5 | async-start | bytes 2097152 | tf_op jit(solution)/shard_map/all_to_all | solution.py:78
  156.0 4.2 fusion.22
  160.3 4.6 fusion.69
  164.9 1.6 dot_general.158
  166.6 4.1 fusion.24
  170.7 1.4 copy.51
  172.0 2.4 reshape.262
  174.4 4.6 all-to-all-done.5
  179.0 6.8 %all-to-all-start.1 = ((bf16[16,5,4096]{2,1,0:T(8,128)(2,1)}), bf16[16,5,4096]{2,1,0:T(8,128)(2,1)}, u32[]{:S(2)}, u32[]{:S(2)}) async-start(bf16[16,5,4096]{2,1,0:T(8,128)(2,1)} %copy.51), calls=%async_computation.1 | async-start | bytes 2097152 | tf_op jit(solution)/shard_map/all_to_all | solution.py:78
  185.8 4.2 fusion.20
  190.1 4.7 fusion.66
  194.7 1.6 dot_general.167
  196.3 4.1 fusion.27
  200.5 1.4 copy.60
  201.9 2.4 reshape.264
  204.2 4.5 all-to-all-done.1
  208.7 6.8 %all-to-all-start.3 = ((bf16[16,5,4096]{2,1,0:T(8,128)(2,1)}), bf16[16,5,4096]{2,1,0:T(8,128)(2,1)}, u32[]{:S(2)}, u32[]{:S(2)}) async-start(bf16[16,5,4096]{2,1,0:T(8,128)(2,1)} %copy.60), calls=%async_computation.3 | async-start | bytes 2097152 | tf_op jit(solution)/shard_map/all_to_all | solution.py:78
  215.6 4.2 fusion.16
  219.8 4.6 fusion.60
  224.5 1.6 dot_general.185
  226.1 4.1 fusion.33
  231.7 2.9 fusion.43
  234.6 3.9 all-to-all-done.3
  238.5 6.8 %all-to-all-start.7 = ((bf16[16,5,4096]{2,1,0:T(8,128)(2,1)}), bf16[16,5,4096]{2,1,0:T(8,128)(2,1)}, u32[]{:S(2)}, u32[]{:S(2)}) async-start(bf16[16,5,4096]{2,1,0:T(8,128)(2,1)} %copy.78), calls=%async_computation.7 | async-start | bytes 2097152 | tf_op jit(solution)/shard_map/all_to_all | solution.py:78
  246.9 2.3 fusion.42
  250.2 2.3 fusion.41
  253.5 14.8 %all-to-all-done.7 = bf16[16,5,4096]{2,1,0:T(8,128)(2,1)} async-done(((bf16[16,5,4096]{2,1,0:T(8,128)(2,1)}), bf16[16,5,4096]{2,1,0:T(8,128)(2,1)}, u32[]{:S(2)}, u32[]{:S(2)}) %all-to-all-start.7) | async-done | bytes 655392 | tf_op jit(solution)/shard_map/all_to_all | solution.py:78
  268.3 2.3 fusion.40
  271.0 1.5 fusion.172
  272.5 24.7 %all-gather.3 = bf16[16,2,4096]{2,1,0:T(2,128)(2,1)} all-gather(bf16[1,2,4096]{2,1,0:T(2,128)(2,1)S(1)} %get-tuple-element.27), channel_id=1, replica_groups=mesh['groups'=2,'expert'=4,'tensor'=4,'sub'=1] {'expert','tensor'}, dimensions={0}, use_global_device_ids=true | all-gather | bytes 278528 | tf_op jit(solution)/shard_map/all_gather | solution.py:93
  298.2 19.8 %all-gather.2 = bf16[16,2,4096]{2,1,0:T(2,128)(2,1)} all-gather(bf16[1,2,4096]{2,1,0:T(2,128)(2,1)} %get-tuple-element.26), channel_id=1, replica_groups=mesh['groups'=2,'expert'=4,'tensor'=4,'sub'=1] {'expert','tensor'}, dimensions={0}, use_global_device_ids=true | all-gather | bytes 278528 | tf_op jit(solution)/shard_map/all_gather | solution.py:93
  318.0 1.8 reshape.274
  319.7 3.2 fusion.221
  324.1 4.1 fusion.76
  328.2 4.1 fusion.77
  332.4 20.8 %all-gather.1 = bf16[16,2,4096]{2,1,0:T(2,128)(2,1)} all-gather(bf16[1,2,4096]{2,1,0:T(2,128)(2,1)S(1)} %copy-done.13), channel_id=1, replica_groups=mesh['groups'=2,'expert'=4,'tensor'=4,'sub'=1] {'expert','tensor'}, dimensions={0}, use_global_device_ids=true | all-gather | bytes 278528 | tf_op jit(solution)/shard_map/all_gather | solution.py:93
  354.3 3.1 fusion.219
  357.3 4.1 fusion.78
  361.5 19.6 %all-gather = bf16[16,2,4096]{2,1,0:T(2,128)(2,1)} all-gather(bf16[1,2,4096]{2,1,0:T(2,128)(2,1)S(1)} %get-tuple-element.24), channel_id=1, replica_groups=mesh['groups'=2,'expert'=4,'tensor'=4,'sub'=1] {'expert','tensor'}, dimensions={0}, use_global_device_ids=true | all-gather | bytes 278528 | tf_op jit(solution)/shard_map/all_gather | solution.py:93
  382.1 3.1 fusion.218
  385.1 4.1 fusion.79
  392.7 93.3 %all-reduce.7.cloned.1.call-done = (f32[32,4096]{1,0:T(8,128)}, f32[32,4096]{1,0:T(8,128)}, f32[32,4096]{1,0:T(8,128)}, f32[32,4096]{1,0:T(8,128)}) async-done(((f32[32,4096]{1,0:T(8,128)}, f32[32,4096]{1,0:T(8,128)}, f32[32,4096]{1,0:T(8,128)}, f32[32,4096]{1,0:T(8,128)}), (f32[32,4096]{1,0:T(8,128)}, f32[32,4096]{1,0:T(8,128)}, f32[32,4096]{1,0:T(8,128)}, ...) | async-done | bytes 2097168
  (166 shorter events, 61.3 us)
Async XLA Ops:
  7.2 317.0 %copy-start = (bf16[384,4096]{1,0:T(8,128)(2,1)S(1)}, bf16[384,4096]{1,0:T(8,128)(2,1)}, u32[]{:S(2)}) copy-start(bf16[384,4096]{1,0:T(8,128)(2,1)} %param.24) | copy-start | bytes 9437188
  9.1 13.5 %copy-start.12 = (f32[4096]{0:T(1024)S(1)}, f32[4096]{0:T(1024)}, u32[]{:S(2)}) copy-start(f32[4096]{0:T(1024)} %param.16) | copy-start | bytes 49156
  9.4 14.4 %copy-start.21 = (f32[10,8]{1,0:T(8,128)}, f32[10,8]{1,0:T(8,128)S(1)}, u32[]{:S(2)}) copy-start(f32[10,8]{1,0:T(8,128)S(1)} %eq.248) | copy-start | bytes 964
  15.2 45.4 %all-to-all-start.6 = ((bf16[16,5,4096]{2,1,0:T(8,128)(2,1)}), bf16[16,5,4096]{2,1,0:T(8,128)(2,1)}, u32[]{:S(2)}, u32[]{:S(2)}) async-start(bf16[16,5,4096]{2,1,0:T(8,128)(2,1)} %copy.76), calls=%async_computation.6 | async-start | bytes 2097152 | tf_op jit(solution)/shard_map/all_to_all | solution.py:66
  24.7 7.5 %copy-start.14 = (s32[10,8]{1,0:T(8,128)}, s32[10,8]{1,0:T(8,128)S(1)}, u32[]{:S(2)}) copy-start(s32[10,8]{1,0:T(8,128)S(1)} %copy.65) | copy-start | bytes 964
  24.9 0.5 copy-start.26
  28.2 6.9 %copy-start.19 = (s32[10,8]{0,1:T(8,128)S(1)}, s32[10,8]{0,1:T(8,128)}, u32[]{:S(2)}) copy-start(s32[10,8]{0,1:T(8,128)} %get-tuple-element.30) | copy-start | bytes 964
  28.2 7.6 %copy-start.18 = (s32[1,10,8]{1,2,0:T(8,128)S(1)}, s32[1,10,8]{1,2,0:T(8,128)}, u32[]{:S(2)}) copy-start(s32[1,10,8]{1,2,0:T(8,128)} %get-tuple-element.33) | copy-start | bytes 964
  36.0 0.6 copy-start.27
  40.2 6.9 %copy-start.22 = (f32[10,8]{1,0:T(8,128)}, f32[10,8]{1,0:T(8,128)S(1)}, u32[]{:S(2)}) copy-start(f32[10,8]{1,0:T(8,128)S(1)} %eq.224) | copy-start | bytes 964
  41.4 5.7 %copy-start.32 = (f32[10]{0:T(128)}, f32[10]{0:T(128)S(1)}, u32[]{:S(2)}) copy-start(f32[10]{0:T(128)S(1)} %add_rsqrt_fusion.10) | copy-start | bytes 124
  47.1 0.5 copy-start.25
  50.6 8.4 %copy-start.16 = (s32[10,8]{1,0:T(8,128)S(1)}, s32[10,8]{1,0:T(8,128)}, u32[]{:S(2)}) copy-start(s32[10,8]{1,0:T(8,128)} %copy.56) | copy-start | bytes 964
  50.6 8.8 %copy-start.17 = (s32[10,8]{1,0:T(8,128)S(1)}, s32[10,8]{1,0:T(8,128)}, u32[]{:S(2)}) copy-start(s32[10,8]{1,0:T(8,128)} %copy.47) | copy-start | bytes 964
  51.3 4.8 copy-start.23
  51.3 7.8 %copy-start.7 = (bf16[1,10,4096]{2,0,1:T(2,128)(2,1)S(1)}, bf16[1,10,4096]{2,0,1:T(2,128)(2,1)}, u32[]{:S(2)}) copy-start(bf16[1,10,4096]{2,0,1:T(2,128)(2,1)} %get-tuple-element.16) | copy-start | bytes 245764
  51.3 7.8 %copy-start.33 = (bf16[4096,16]{0,1:T(8,128)(2,1)S(1)}, bf16[4096,16]{0,1:T(8,128)(2,1)}, u32[]{:S(2)}) copy-start(bf16[4096,16]{0,1:T(8,128)(2,1)} %param.17) | copy-start | bytes 393220
  54.7 43.5 %copy-start.15 = (s32[10,8]{1,0:T(8,128)S(1)}, s32[10,8]{1,0:T(8,128)}, u32[]{:S(2)}) copy-start(s32[10,8]{1,0:T(8,128)} %copy-done.14) | copy-start | bytes 964
  59.4 41.9 %copy-start.24 = (f32[10,8]{1,0:T(8,128)S(1)}, f32[10,8]{1,0:T(8,128)}, u32[]{:S(2)}) copy-start(f32[10,8]{1,0:T(8,128)} %copy-done.23) | copy-start | bytes 964
  60.6 29.0 %all-to-all-start.4 = ((bf16[16,5,4096]{2,1,0:T(8,128)(2,1)}), bf16[16,5,4096]{2,1,0:T(8,128)(2,1)}, u32[]{:S(2)}, u32[]{:S(2)}) async-start(bf16[16,5,4096]{2,1,0:T(8,128)(2,1)} %copy.67), calls=%async_computation.4 | async-start | bytes 2097152 | tf_op jit(solution)/shard_map/all_to_all | solution.py:66
  89.6 29.8 %all-to-all-start = ((bf16[16,5,4096]{2,1,0:T(8,128)(2,1)}), bf16[16,5,4096]{2,1,0:T(8,128)(2,1)}, u32[]{:S(2)}, u32[]{:S(2)}) async-start(bf16[16,5,4096]{2,1,0:T(8,128)(2,1)} %copy.49), calls=%async_computation | async-start | bytes 2097152 | tf_op jit(solution)/shard_map/all_to_all | solution.py:66
  119.4 29.8 %all-to-all-start.2 = ((bf16[16,5,4096]{2,1,0:T(8,128)(2,1)}), bf16[16,5,4096]{2,1,0:T(8,128)(2,1)}, u32[]{:S(2)}, u32[]{:S(2)}) async-start(bf16[16,5,4096]{2,1,0:T(8,128)(2,1)} %copy.58), calls=%async_computation.2 | async-start | bytes 2097152 | tf_op jit(solution)/shard_map/all_to_all | solution.py:66
  126.2 4.3 copy-start.2
  149.2 29.8 %all-to-all-start.5 = ((bf16[16,5,4096]{2,1,0:T(8,128)(2,1)}), bf16[16,5,4096]{2,1,0:T(8,128)(2,1)}, u32[]{:S(2)}, u32[]{:S(2)}) async-start(bf16[16,5,4096]{2,1,0:T(8,128)(2,1)} %copy.69), calls=%async_computation.5 | async-start | bytes 2097152 | tf_op jit(solution)/shard_map/all_to_all | solution.py:78
  156.0 4.3 copy-start.3
  179.0 29.8 %all-to-all-start.1 = ((bf16[16,5,4096]{2,1,0:T(8,128)(2,1)}), bf16[16,5,4096]{2,1,0:T(8,128)(2,1)}, u32[]{:S(2)}, u32[]{:S(2)}) async-start(bf16[16,5,4096]{2,1,0:T(8,128)(2,1)} %copy.51), calls=%async_computation.1 | async-start | bytes 2097152 | tf_op jit(solution)/shard_map/all_to_all | solution.py:78
  185.8 4.3 copy-start.4
  208.7 29.8 %all-to-all-start.3 = ((bf16[16,5,4096]{2,1,0:T(8,128)(2,1)}), bf16[16,5,4096]{2,1,0:T(8,128)(2,1)}, u32[]{:S(2)}, u32[]{:S(2)}) async-start(bf16[16,5,4096]{2,1,0:T(8,128)(2,1)} %copy.60), calls=%async_computation.3 | async-start | bytes 2097152 | tf_op jit(solution)/shard_map/all_to_all | solution.py:78
  215.6 4.3 copy-start.5
  226.1 5.5 %copy-start.8 = (bf16[1,10,4096]{2,0,1:T(2,128)(2,1)S(1)}, bf16[1,10,4096]{2,0,1:T(2,128)(2,1)}, u32[]{:S(2)}) copy-start(bf16[1,10,4096]{2,0,1:T(2,128)(2,1)} %get-tuple-element.16) | copy-start | bytes 245764
  226.1 5.5 %copy-start.35 = (f32[16,5,10]{0,1,2:T(8,128)S(1)}, f32[16,5,10]{0,1,2:T(8,128)}, u32[]{:S(2)}) copy-start(f32[16,5,10]{0,1,2:T(8,128)} %convolution_bitcast_fusion.7) | copy-start | bytes 9604
  230.3 15.4 %copy-start.31 = (s32[2]{0:T(128)S(1)}, s32[2]{0:T(128)}, u32[]{:S(2)}) copy-start(s32[2]{0:T(128)} %fusion.195) | copy-start | bytes 28
  230.3 18.9 %copy-start.29 = (s32[2]{0:T(128)S(1)}, s32[2]{0:T(128)}, u32[]{:S(2)}) copy-start(s32[2]{0:T(128)} %fusion.194) | copy-start | bytes 28
  231.7 21.5 %copy-start.30 = (s32[2]{0:T(128)S(1)}, s32[2]{0:T(128)}, u32[]{:S(2)}) copy-start(s32[2]{0:T(128)} %fusion.193) | copy-start | bytes 28
  234.6 36.0 %copy-start.28 = (s32[2]{0:T(128)S(1)}, s32[2]{0:T(128)}, u32[]{:S(2)}) copy-start(s32[2]{0:T(128)} %fusion.192) | copy-start | bytes 28
  238.5 29.8 %all-to-all-start.7 = ((bf16[16,5,4096]{2,1,0:T(8,128)(2,1)}), bf16[16,5,4096]{2,1,0:T(8,128)(2,1)}, u32[]{:S(2)}, u32[]{:S(2)}) async-start(bf16[16,5,4096]{2,1,0:T(8,128)(2,1)} %copy.78), calls=%async_computation.7 | async-start | bytes 2097152 | tf_op jit(solution)/shard_map/all_to_all | solution.py:78
  245.4 240.6 %all-reduce.7.cloned.1.call-start = ((), (), s32[]{:S(2)}) async-start(), calls=%async_computation.8 | async-start | bytes 4194304
  249.2 3.3 copy-start.9
  252.5 0.7 copy-start.10
  270.6 1.8 copy-start.11
  319.7 3.2 copy-start.1
  319.7 3.2 copy-start.6
  328.2 4.1 copy-start.13
  385.1 4.2 copy-start.34
  389.3 101.1 %copy-start.20 = (f32[4096]{0:T(1024)S(1)}, f32[4096]{0:T(1024)}, u32[]{:S(2)}) copy-start(f32[4096]{0:T(1024)} %param.25) | copy-start | bytes 49156
Sparse Core Ops, SparseCore 0:
  389.4 96.5 all-reduce.6
where the time goes:
time: 502 us; the launch traced here: 499 us
  waiting for transfers between devices  159 us (32%)
  matrix products  107 us (21%)
  blocking collectives  84.8 us (17%)
  starting transfers between devices  54.8 us (11%)
  local copies, waits for them, and re-layouts  48.1 us (10%)
  other arithmetic  29.9 us (6%)
  between operations  15.1 us (3%)
    unnamed x2, waiting for transfers between devices  93.3 us
    all_gather x4, blocking collectives, local(): lax.all_gather(draft_input, ('expert', 'tensor'), axis=0, tiled=True)  84.8 us
    all_to_all x4, waiting for transfers between devices, local(): lax.all_to_all(outgoing, ('expert', 'tensor'), split_axis=0, concat_axis=...  37.7 us
    all_to_all x4, waiting for transfers between devices, local(): lax.all_to_all(processed, ('expert', 'tensor'), split_axis=0, concat_axis...  27.9 us
    all_to_all x4, starting transfers between devices, local(): lax.all_to_all(processed, ('expert', 'tensor'), split_axis=0, concat_axis...  27.4 us
    all_to_all x4, starting transfers between devices, local(): lax.all_to_all(outgoing, ('expert', 'tensor'), split_axis=0, concat_axis=...  27.1 us
    dot_general x4, matrix products, local(): jnp.dot(flat_rows, up_weight[0], preferred_element_type=jnp.float32)  18.6 us
    dot_general x4, matrix products, local(): jnp.dot(flat_rows, gate_weight[0], preferred_element_type=jnp.float32)  17 us
  transfers between devices with their start and end apart: 9, of which 8 were waited for; matrix products, arithmetic and copies ran while one was open for 27% of the time, Pallas kernels for 0%

commit v1 on v0

v1 whole, which is shorter than its diff:
```python
import jax
import jax.numpy as jnp
from jax import lax
from jax.sharding import PartitionSpec as P

EPSILON = 1e-06
RING = ("expert", "tensor")


def rms_scale(values, weights):
    values = values.astype(jnp.float32)
    mean_square = jnp.mean(values * values, axis=-1, keepdims=True)
    return values * lax.rsqrt(mean_square + EPSILON) * weights


def local(
    hidden_rows,
    expert_ids,
    accepted,
    norm_gain,
    router,
    gate_weight,
    up_weight,
    down_weight,
    draft_gain,
    draft_gate,
    draft_up,
    draft_down,
    final_gain,
):
    rounds_total, rows_here, width = hidden_rows.shape
    expert_count = router.shape[1]
    requests_here = accepted.shape[1]
    draft_rows = rows_here // requests_here
    total = rounds_total * rows_here
    my_expert = lax.axis_index(RING)

    rows = hidden_rows.reshape(total, width).astype(jnp.float32)
    normed = rms_scale(rows, norm_gain).astype(jnp.bfloat16)
    logits = jnp.dot(normed, router, preferred_element_type=jnp.float32)
    ids = expert_ids.reshape(total, -1)
    named = jnp.any(ids[:, :, None] == jnp.arange(expert_count, dtype=jnp.int32), axis=1)
    weights = jnp.where(named, jnp.exp(logits), 0.0)
    table = weights / jnp.sum(weights, axis=1, keepdims=True)

    everyone = lax.all_gather(normed, RING, axis=0, tiled=True)
    table = lax.all_gather(table, RING, axis=0, tiled=True)
    share = jnp.sum(
        jnp.where(jnp.arange(expert_count) == my_expert, table, 0.0), axis=1, keepdims=True
    )
    gate_values = jnp.dot(everyone, gate_weight[0], preferred_element_type=jnp.float32)
    up_values = jnp.dot(everyone, up_weight[0], preferred_element_type=jnp.float32)
    active = (jax.nn.silu(gate_values) * up_values).astype(jnp.bfloat16)
    part = jnp.dot(active, down_weight[0], preferred_element_type=jnp.float32)
    part = (share * part).astype(jnp.bfloat16)
    mixed = lax.psum_scatter(part, RING, scatter_dimension=0, tiled=True)
    mixed = lax.psum(mixed, "sub").astype(jnp.float32)
    verified = (rows + mixed).astype(jnp.bfloat16)

    by_request = verified.reshape(rounds_total, requests_here, draft_rows, width)
    pick = jnp.arange(draft_rows, dtype=jnp.int32) == accepted[:, :, None]
    features = jnp.sum(jnp.where(pick[..., None], by_request.astype(jnp.float32), 0.0), axis=2)
    features = features.reshape(rounds_total * requests_here, width)
    draft_input = rms_scale(features, draft_gain).astype(jnp.bfloat16)
    pieces = lax.all_gather(draft_input, RING, axis=0, tiled=True)
    gate_part = jnp.dot(pieces, draft_gate, preferred_element_type=jnp.float32)
    up_part = jnp.dot(pieces, draft_up, preferred_element_type=jnp.float32)
    units = (jax.nn.silu(gate_part) * up_part).astype(jnp.bfloat16)
    summed = lax.psum_scatter(
        jnp.dot(units, draft_down, preferred_element_type=jnp.float32).astype(jnp.bfloat16),
        RING,
        scatter_dimension=0,
        tiled=True,
    ).astype(jnp.float32)
    draft_out = rms_scale(features + summed, final_gain).astype(jnp.bfloat16)
    return (
        verified.reshape(hidden_rows.shape),
        draft_out.reshape(rounds_total, requests_here, width),
    )


def solution(mesh):
    placed = (
        P(None, ("groups", "expert", "tensor"), None),
        P(None, ("groups", "expert", "tensor"), None),
        P(None, ("groups", "expert", "tensor")),
        P(),
        P(),
        P(("expert", "tensor"), None, "sub"),
        P(("expert", "tensor"), None, "sub"),
        P(("expert", "tensor"), "sub", None),
        P(),
        P(None, ("expert", "tensor")),
        P(None, ("expert", "tensor")),
        P(("expert", "tensor"), None),
        P(),
    )
    return jax.shard_map(
        local,
        mesh=mesh,
        in_specs=placed,
        out_specs=(
            P(None, ("groups", "expert", "tensor"), None),
            P(None, ("groups", "expert", "tensor"), None),
        ),
        check_vma=False,
    )
```

time: 502 us -> 301 us (0.60)
  matrix products: 107 us -> 37.7 us
  blocking collectives: 84.8 us -> 24 us
  starting transfers between devices: 54.8 us -> 0.34 us
  waiting for transfers between devices: 159 us -> 200 us
  local copies, waits for them, and re-layouts: 48.1 us -> 12.8 us
  other arithmetic: 29.9 us -> 11.7 us
    reduce_scatter x0 -> x2, waiting for transfers between devices: none -> 130 us  [the longest x1 76.3 us: local(): mixed = lax.psum_scatter(part, RING, scatter_dimension=0, tiled=True)]
    unnamed x2 -> x4, waiting for transfers between devices: 93.3 us -> 0.07 us
    all_gather x0 -> x2, waiting for transfers between devices: none -> 69.5 us  [the longest x1 36.9 us: local(): pieces = lax.all_gather(draft_input, RING, axis=0, tiled=True)]
    dot_general x40 -> x4, matrix products: 104 us -> 36.5 us  [the longest x1 18.5 us: local(): part = jnp.dot(active, down_weight[0], preferred_element_type=jnp.float32)]
    all_to_all x8 -> x0, waiting for transfers between devices: 65.6 us -> none  [the longest x4 37.7 us: local(): lax.all_to_all(outgoing, ('expert', 'tensor'), split_axis=0, concat_axis=...]
    all_gather x4 -> x1, blocking collectives: 84.8 us -> 24 us  [local(): table = lax.all_gather(table, RING, axis=0, tiled=True)]
    all_to_all x8 -> x0, starting transfers between devices: 54.5 us -> none  [the longest x4 27.4 us: local(): lax.all_to_all(processed, ('expert', 'tensor'), split_axis=0, concat_axis...]
    slice x7 -> x0, local copies, waits for them, and re-layouts: 6.99 us -> none  [the longest x1 2.9 us: local(): rows = hidden_rows[round_index]]
  transfers between devices with their start and end apart: 9 -> 4, of which waited for: 8 -> 4; matrix products, arithmetic and copies ran while one was open for 27% -> 2% of each run, Pallas kernels for 0% -> 0%
where the time goes in v1:
time: 301 us; the launch traced here: 300 us
  waiting for transfers between devices  200 us (66%)
  matrix products  37.7 us (13%)
  blocking collectives  24 us (8%)
  between operations  13.8 us (5%)
  local copies, waits for them, and re-layouts  12.8 us (4%)
  other arithmetic  11.7 us (4%)
    reduce_scatter x1, waiting for transfers between devices, local(): mixed = lax.psum_scatter(part, RING, scatter_dimension=0, tiled=True)  76.3 us
    reduce_scatter x1, waiting for transfers between devices, local(): lax.psum_scatter(jnp.dot(units, draft_down, preferred_element_type=jnp.fl...  53.7 us
    all_gather x1, waiting for transfers between devices, local(): pieces = lax.all_gather(draft_input, RING, axis=0, tiled=True)  36.9 us
    all_gather x1, waiting for transfers between devices, local(): everyone = lax.all_gather(normed, RING, axis=0, tiled=True)  32.6 us
    all_gather x1, blocking collectives, local(): table = lax.all_gather(table, RING, axis=0, tiled=True)  24 us
    dot_general x1, matrix products, local(): part = jnp.dot(active, down_weight[0], preferred_element_type=jnp.float32)  18.5 us
    dot_general x1, matrix products, local(): jnp.dot(everyone, gate_weight[0], preferred_element_type=jnp.float32)  9.83 us
  transfers between devices with their start and end apart: 4, of which 4 were waited for; matrix products, arithmetic and copies ran while one was open for 2% of the time, Pallas kernels for 0%

profile of v1, /device:TPU:0, one launch (start us, length us, event | category | flops | bytes accessed | tf_op | source)
XLA Modules:
  0.0 299.9 jit_solution(18209610796333644949)
XLA Ops:
  7.2 0.0 copy-start
  7.2 0.0 all-gather.4.cloned.1.call-start
  7.2 2.3 copy.37
  9.5 1.2 multiply_reduce_fusion
  10.8 2.2 reshape.74
  13.0 0.1 copy.43
  13.1 0.1 rsqrt.31
  13.1 1.9 multiply_convert_fusion.2
  15.1 0.0 all-gather.4.cloned.1.call-update
  15.1 0.0 reduce-scatter.3.cloned.1.call-start
  15.2 0.7 copy.38
  15.9 0.1 eq.40
  16.0 1.2 fusion.21
  17.2 24.0 %all-gather = f32[16,40,16]{1,2,0:T(8,128)S(1)} all-gather(f32[1,40,16]{1,2,0:T(8,128)S(1)} %divide_bitcast_fusion), channel_id=1, replica_groups=mesh['groups'=2,'expert'=4,'tensor'=4,'sub'=1] {'expert','tensor'}, dimensions={0}, use_global_device_ids=true | all-gather | bytes 43520 | tf_op jit(solution)/shard_map/all_gather | solution.py:47
  41.3 0.1 reshape.77
  41.4 0.1 select_reduce_fusion.1
  41.5 32.6 %all-gather.4.cloned.1.call-done = bf16[640,4096]{1,0:T(8,128)(2,1)} async-done(((bf16[40,4096]{1,0:T(8,128)(2,1)}), bf16[640,4096]{1,0:T(8,128)(2,1)}) %all-gather.4.cloned.1.call-update) | async-done | bytes 5242896 | tf_op jit(solution)/shard_map/all_gather | solution.py:46
  74.1 9.8 %fusion.3 = f32[640,768]{1,0:T(8,128)} fusion(bf16[640,4096]{1,0:T(8,128)(2,1)} %all-gather.4.cloned.1.call-done, bf16[1,4096,768]{2,1,0:T(8,128)(2,1)} %param.18), kind=kOutput, calls=%fused_computation.4 | convolution fusion | flops 4026531840 | bytes 13500416 | tf_op jit(solution)/shard_map/dot_general | solution.py:51
  83.9 18.5 %multiply_convert_fusion = bf16[640,4096]{1,0:T(8,128)(2,1)} fusion(bf16[1,768,4096]{2,1,0:T(8,128)(2,1)} %param.20, f32[640]{0:T(1024)S(1)} %select_reduce_fusion.1, f32[640,768]{1,0:T(8,128)} %fusion.3, bf16[640,4096]{1,0:T(8,128)(2,1)} %all-gather.4.cloned.1.call-done, bf16[1,4096,768]{2,1,0:T(8,128)(2,1)} %param.19), kind=kOutput, calls=%fused_computation | convolution fusion | flops 8061255680 | bytes 25037312 | tf_op jit(solution)/shard_map/dot_general | solution.py:54
  102.4 0.0 copy-start.3
  102.4 0.0 copy-start.2
  102.4 0.0 reduce-scatter.3.cloned.1.call-update
  102.4 0.0 all-gather.6.cloned.1.call-start
  102.4 0.6 copy-done.3
  103.0 0.1 copy.41
  103.1 0.1 iota_compare_fusion.1
  103.2 76.3 %reduce-scatter.3.cloned.1.call-done = bf16[40,4096]{1,0:T(8,128)(2,1)} async-done(((bf16[640,4096]{1,0:T(8,128)(2,1)}), bf16[40,4096]{1,0:T(8,128)(2,1)}) %reduce-scatter.3.cloned.1.call-update) | async-done | bytes 327696 | tf_op jit(solution)/shard_map/reduce_scatter | solution.py:56
  179.5 1.2 add_convert_fusion
  180.8 1.1 reshape.75
  181.9 2.4 select_reduce_fusion
  184.2 1.6 reshape.72
  185.9 1.1 multiply_reduce_fusion.2
  186.9 0.1 rsqrt.33
  187.0 0.0 copy-done.2
  187.0 1.6 multiply_convert_fusion.4
  188.6 0.0 all-gather.6.cloned.1.call-update
  188.7 0.2 reduce-scatter.5.cloned.1.call-start
  188.9 36.9 %all-gather.6.cloned.1.call-done = bf16[128,4096]{1,0:T(8,128)(2,1)} async-done(((bf16[8,4096]{1,0:T(8,128)(2,1)}), bf16[128,4096]{1,0:T(8,128)(2,1)}) %all-gather.6.cloned.1.call-update) | async-done | bytes 1048592 | tf_op jit(solution)/shard_map/all_gather | solution.py:65
  225.8 3.6 %fusion.22 = f32[128,384]{1,0:T(8,128)} fusion(bf16[128,4096]{1,0:T(8,128)(2,1)} %all-gather.6.cloned.1.call-done, bf16[4096,384]{1,0:T(8,128)(2,1)} %param.22), kind=kOutput, calls=%fused_computation.40 | convolution fusion | flops 402653184 | bytes 4390912 | tf_op jit(solution)/shard_map/dot_general | solution.py:66
  229.4 0.0 copy-done
  229.4 0.0 copy-start.1
  229.4 4.6 %convolution_convert_fusion = bf16[128,4096]{1,0:T(8,128)(2,1)} fusion(bf16[384,4096]{1,0:T(8,128)(2,1)S(1)} %copy-done, bf16[128,4096]{1,0:T(8,128)(2,1)} %all-gather.6.cloned.1.call-done, bf16[4096,384]{1,0:T(8,128)(2,1)} %param.23, f32[128,384]{1,0:T(8,128)} %fusion.22), kind=kOutput, calls=%fused_computation.6 | convolution fusion | flops 806125568 | bytes 8585216 | tf_op jit(solution)/shard_map/dot_general | solution.py:70
  234.0 0.0 reduce-scatter.5.cloned.1.call-update
  234.0 0.9 reshape.71
  234.9 2.0 copy.42
  237.0 53.7 %reduce-scatter.5.cloned.1.call-done = bf16[8,4096]{1,0:T(8,128)(2,1)} async-done(((bf16[128,4096]{1,0:T(8,128)(2,1)}), bf16[8,4096]{1,0:T(8,128)(2,1)}) %reduce-scatter.5.cloned.1.call-update) | async-done | bytes 65552 | tf_op jit(solution)/shard_map/reduce_scatter | solution.py:69
  290.7 1.1 multiply_reduce_fusion.1
  291.7 0.0 copy-done.1
  291.7 1.0 multiply_convert_fusion.3
  292.7 0.7 reshape.73
  (7 shorter events, 0.1 us)
Async XLA Ops:
  7.2 222.2 %copy-start = (bf16[384,4096]{1,0:T(8,128)(2,1)S(1)}, bf16[384,4096]{1,0:T(8,128)(2,1)}, u32[]{:S(2)}) copy-start(bf16[384,4096]{1,0:T(8,128)(2,1)} %param.24) | copy-start | bytes 9437188
  7.2 66.9 %all-gather.4.cloned.1.call-start = ((), (), s32[]{:S(2)}) async-start(), calls=%async_computation.2 | async-start | bytes 5570560 | tf_op jit(solution)/shard_map/all_gather | solution.py:46
  15.1 164.4 %reduce-scatter.3.cloned.1.call-start = ((), (), s32[]{:S(2)}) async-start(), calls=%async_computation.3 | async-start | bytes 5570560 | tf_op jit(solution)/shard_map/reduce_scatter | solution.py:56
  102.4 0.7 copy-start.3
  102.4 84.7 %copy-start.2 = (f32[4096]{0:T(1024)S(1)}, f32[4096]{0:T(1024)}, u32[]{:S(2)}) copy-start(f32[4096]{0:T(1024)} %param.21) | copy-start | bytes 49156
  102.4 123.4 %all-gather.6.cloned.1.call-start = ((), (), s32[]{:S(2)}) async-start(), calls=%async_computation.4 | async-start | bytes 1114112 | tf_op jit(solution)/shard_map/all_gather | solution.py:65
  188.7 102.0 %reduce-scatter.5.cloned.1.call-start = ((), (), s32[]{:S(2)}) async-start(), calls=%async_computation.5 | async-start | bytes 1114112 | tf_op jit(solution)/shard_map/reduce_scatter | solution.py:69
  229.4 62.3 %copy-start.1 = (f32[4096]{0:T(1024)S(1)}, f32[4096]{0:T(1024)}, u32[]{:S(2)}) copy-start(f32[4096]{0:T(1024)} %param.25) | copy-start | bytes 49156
Sparse Core Ops, SparseCore 0:
  15.2 58.7 all-gather.3
  102.5 76.9 reduce-scatter.2
  188.8 36.9 all-gather.5
  234.1 56.4 reduce-scatter.4

commit v2 on v1

--- a/solution.py
+++ b/solution.py
@@ -1,10 +1,253 @@
+import functools
+
 import jax
 import jax.numpy as jnp
 from jax import lax
+from jax.experimental import pallas as pl
+from jax.experimental.pallas import tpu as pltpu
 from jax.sharding import PartitionSpec as P
 
 EPSILON = 1e-06
 RING = ("expert", "tensor")
+MESH = pl.DeviceIdType.MESH
+
+
+class Loop:
+    def __init__(self, mesh_shape):
+        self.expert, self.tensor = mesh_shape["expert"], mesh_shape["tensor"]
+        two = mesh_shape["sub"] == 1 and self.tensor % 2 == 0
+        self.lanes = 2 if two else 1
+        self.n = self.expert * self.tensor // self.lanes
+        self.half = self.n // 2
+
+    def me(self):
+        z, t = lax.axis_index("expert"), lax.axis_index("tensor")
+        x, lane = lax.div(t, self.lanes), lax.rem(t, self.lanes)
+        flip = lax.rem(x, 2)
+        return x * self.expert + z + flip * (self.expert - 1 - 2 * z), lane
+
+    def at(self, position, lane):
+        q = lax.rem(position + self.n, self.n)
+        x, z = lax.div(q, self.expert), lax.rem(q, self.expert)
+        z = z + lax.rem(x, 2) * (self.expert - 1 - 2 * z)
+        return z, x * self.lanes + lane
+
+    def device(self, position, lane):
+        z, t = self.at(position, lane)
+        return {"expert": z, "tensor": t}
+
+    def block(self, position, lane):
+        z, t = self.at(position, lane)
+        return z * self.tensor + t
+
+    def greet(self, p, lane):
+        barrier = pltpu.get_barrier_semaphore()
+        others = [self.device(p + 1, lane), self.device(p - 1, lane)]
+        if self.lanes == 2:
+            others.append(self.device(p, 1 - lane))
+        for other in others:
+            pl.semaphore_signal(barrier, inc=1, device_id=other, device_id_type=MESH)
+        pl.semaphore_wait(barrier, len(others))
+
+
+def gather_kernel(loop, pieces, inputs, *refs):
+    sources, outs = refs[:inputs], refs[inputs : 2 * inputs]
+    ring_send, ring_recv, pair_send, pair_recv, own_sem = refs[2 * inputs :]
+    p, lane = loop.me()
+    last = loop.half
+    loop.greet(p, lane)
+
+    def source(c):
+        which, start, size = pieces[c]
+        return sources[which].at[:, pl.ds(start, size)]
+
+    def landed(block, c):
+        which, start, size = pieces[c]
+        return outs[which].at[block, :, pl.ds(start, size)]
+
+    def used(way, step, c):
+        return step < last or c % 2 == way
+
+    started, ring = [], {}
+
+    def send(way, step, c):
+        q = p - (step - 1) if way == 0 else p + (step - 1)
+        block = loop.block(q, lane)
+        ring[way, step, c] = pltpu.make_async_remote_copy(
+            src_ref=source(c) if step == 1 else landed(block, c),
+            dst_ref=landed(block, c),
+            send_sem=ring_send.at[way, step - 1, c],
+            recv_sem=ring_recv.at[way, step - 1, c],
+            device_id=loop.device(p + 1 if way == 0 else p - 1, lane),
+            device_id_type=MESH,
+        )
+        ring[way, step, c].start()
+
+    def share(k, q, c):
+        if loop.lanes == 1:
+            return
+        block = loop.block(q, lane)
+        copy = pltpu.make_async_remote_copy(
+            src_ref=source(c) if k == 0 else landed(block, c),
+            dst_ref=landed(block, c),
+            send_sem=pair_send.at[k, c],
+            recv_sem=pair_recv.at[k, c],
+            device_id=loop.device(p, 1 - lane),
+            device_id_type=MESH,
+        )
+        copy.start()
+        started.append(copy)
+
+    count = len(pieces)
+    for c in range(count):
+        for way in range(2):
+            if used(way, 1, c):
+                send(way, 1, c)
+    keep = []
+    for c in range(count):
+        share(0, p, c)
+        copy = pltpu.make_async_copy(source(c), landed(loop.block(p, lane), c), own_sem.at[c])
+        copy.start()
+        keep.append(copy)
+    for step in range(2, last + 2):
+        for c in range(count):
+            for way in range(2):
+                if not used(way, step - 1, c):
+                    continue
+                ring[way, step - 1, c].wait_recv()
+                if step <= last and used(way, step, c):
+                    send(way, step, c)
+                q = p - (step - 1) if way == 0 else p + (step - 1)
+                share(way * last + step - 1, q, c)
+    for copy in keep:
+        copy.wait()
+    for copy in ring.values():
+        copy.wait_send()
+    for copy in started:
+        copy.wait()
+
+
+def gather(loop, collective_id, *arrays):
+    pieces = []
+    for which, array in enumerate(arrays):
+        width = array.shape[1]
+        cuts = 2 if width >= 1024 else 1
+        for cut in range(cuts):
+            pieces.append((which, cut * width // cuts, width // cuts))
+    blocks = loop.n * loop.lanes
+    count = len(pieces)
+    return pl.pallas_call(
+        functools.partial(gather_kernel, loop, pieces, len(arrays)),
+        out_shape=[jax.ShapeDtypeStruct((blocks,) + a.shape, a.dtype) for a in arrays],
+        in_specs=[pl.BlockSpec(memory_space=pltpu.VMEM)] * len(arrays),
+        out_specs=[pl.BlockSpec(memory_space=pl.ANY)] * len(arrays),
+        scratch_shapes=[
+            pltpu.SemaphoreType.DMA((2, loop.half, count)),
+            pltpu.SemaphoreType.DMA((2, loop.half, count)),
+            pltpu.SemaphoreType.DMA((2 * loop.half + 1, count)),
+            pltpu.SemaphoreType.DMA((2 * loop.half + 1, count)),
+            pltpu.SemaphoreType.DMA((count,)),
+        ],
+        compiler_params=pltpu.CompilerParams(collective_id=collective_id, has_side_effects=True),
+    )(*arrays)
+
+
+def scatter_kernel(loop, part, out, *refs):
+    if loop.lanes == 2:
+        from_pair, stage, arrived, ring_send, ring_recv, pair_send, pair_recv = refs
+    else:
+        stage, arrived, ring_send, ring_recv = refs
+    p, lane = loop.me()
+    n, last = loop.n, loop.half
+    columns = part.shape[2] // 2
+    loop.greet(p, lane)
+
+    pairs, seen = {}, set()
+    if loop.lanes == 2:
+        for far in range(last, -1, -1):
+            for offset in sorted({far, (n - far) % n}):
+                pairs[offset] = pltpu.make_async_remote_copy(
+                    src_ref=part.at[loop.block(p + offset, 1 - lane)],
+                    dst_ref=from_pair.at[offset],
+                    send_sem=pair_send.at[offset],
+                    recv_sem=pair_recv.at[offset],
+                    device_id=loop.device(p, 1 - lane),
+                    device_id_type=MESH,
+                )
+                pairs[offset].start()
+
+    def mine(offset, h):
+        span = pl.ds(h * columns, columns)
+        value = part[loop.block(p + offset, lane), :, span].astype(jnp.float32)
+        if loop.lanes == 2:
+            if offset not in seen:
+                seen.add(offset)
+                pairs[offset].wait_recv()
+            value = value + from_pair[offset, :, span].astype(jnp.float32)
+        return value
+
+    def used(way, step, h):
+        return 1 <= step <= last and (way == h or step >= 2)
+
+    ring = {}
+    for step in range(1, last + 1):
+        for h in range(2):
+            for way in range(2):
+                if not used(way, step, h):
+                    continue
+                far = last + 1 - step
+                value = mine(far if way == 0 else (n - far) % n, h)
+                if used(way, step - 1, h):
+                    ring[way, step - 1, h].wait_recv()
+                    value = value + arrived[way, step - 2, h].astype(jnp.float32)
+                if used(way, step - 2, h):
+                    ring[way, step - 2, h].wait_send()
+                stage[way, step % 2, h] = value.astype(jnp.bfloat16)
+                ring[way, step, h] = pltpu.make_async_remote_copy(
+                    src_ref=stage.at[way, step % 2, h],
+                    dst_ref=arrived.at[way, step - 1, h],
+                    send_sem=ring_send.at[way, step - 1, h],
+                    recv_sem=ring_recv.at[way, step - 1, h],
+                    device_id=loop.device(p + 1 if way == 0 else p - 1, lane),
+                    device_id_type=MESH,
+                )
+                ring[way, step, h].start()
+    for h in range(2):
+        value = mine(0, h)
+        for way in range(2):
+            if used(way, last, h):
+                ring[way, last, h].wait_recv()
+                value = value + arrived[way, last - 1, h].astype(jnp.float32)
+        out[:, pl.ds(h * columns, columns)] = value
+    for (way, step, h), copy in ring.items():
+        if step >= last - 1:
+            copy.wait_send()
+    for copy in pairs.values():
+        copy.wait_send()
+
+
+def scatter(loop, collective_id, part):
+    blocks, rows, width = part.shape
+    n, last = loop.n, loop.half
+    dma = pltpu.SemaphoreType.DMA
+    scratch = [
+        pltpu.VMEM((2, 2, 2, rows, width // 2), jnp.bfloat16),
+        pltpu.VMEM((2, last, 2, rows, width // 2), jnp.bfloat16),
+        dma((2, last, 2)),
+        dma((2, last, 2)),
+    ]
+    if loop.lanes == 2:
+        scratch = [pltpu.VMEM((n, rows, width), jnp.bfloat16)] + scratch + [dma((n,)), dma((n,))]
+    return pl.pallas_call(
+        functools.partial(scatter_kernel, loop),
+        out_shape=jax.ShapeDtypeStruct((rows, width), jnp.float32),
+        in_specs=[pl.BlockSpec(memory_space=pltpu.VMEM)],
+        out_specs=pl.BlockSpec(memory_space=pltpu.VMEM),
+        scratch_shapes=scratch,
+        compiler_params=pltpu.CompilerParams(
+            collective_id=collective_id, has_side_effects=True, vmem_limit_bytes=60 * 2**20
+        ),
+    )(part)
 
 
 def rms_scale(values, weights):
@@ -14,6 +257,7 @@
 
 
 def local(
+    loop,
     hidden_rows,
     expert_ids,
     accepted,
@@ -43,18 +287,21 @@
     weights = jnp.where(named, jnp.exp(logits), 0.0)
     table = weights / jnp.sum(weights, axis=1, keepdims=True)
 
-    everyone = lax.all_gather(normed, RING, axis=0, tiled=True)
-    table = lax.all_gather(table, RING, axis=0, tiled=True)
+    lanes_wide = -(-expert_count // 128) * 128
+    table = jnp.pad(table, ((0, 0), (0, lanes_wide - expert_count)))
+    everyone, tables = gather(loop, 0, normed, table)
+    everyone = everyone.reshape(-1, width)
     share = jnp.sum(
-        jnp.where(jnp.arange(expert_count) == my_expert, table, 0.0), axis=1, keepdims=True
+        jnp.where(jnp.arange(lanes_wide) == my_expert, tables.reshape(-1, lanes_wide), 0.0),
+        axis=1,
+        keepdims=True,
     )
     gate_values = jnp.dot(everyone, gate_weight[0], preferred_element_type=jnp.float32)
     up_values = jnp.dot(everyone, up_weight[0], preferred_element_type=jnp.float32)
     active = (jax.nn.silu(gate_values) * up_values).astype(jnp.bfloat16)
     part = jnp.dot(active, down_weight[0], preferred_element_type=jnp.float32)
     part = (share * part).astype(jnp.bfloat16)
-    mixed = lax.psum_scatter(part, RING, scatter_dimension=0, tiled=True)
-    mixed = lax.psum(mixed, "sub").astype(jnp.float32)
+    mixed = lax.psum(scatter(loop, 1, part.reshape(-1, total, width)), "sub")
     verified = (rows + mixed).astype(jnp.bfloat16)
 
     by_request = verified.reshape(rounds_total, requests_here, draft_rows, width)
@@ -62,16 +309,13 @@
     features = jnp.sum(jnp.where(pick[..., None], by_request.astype(jnp.float32), 0.0), axis=2)
     features = features.reshape(rounds_total * requests_here, width)
     draft_input = rms_scale(features, draft_gain).astype(jnp.bfloat16)
-    pieces = lax.all_gather(draft_input, RING, axis=0, tiled=True)
+    (pieces,) = gather(loop, 2, draft_input)
+    pieces = pieces.reshape(-1, width)
     gate_part = jnp.dot(pieces, draft_gate, preferred_element_type=jnp.float32)
     up_part = jnp.dot(pieces, draft_up, preferred_element_type=jnp.float32)
     units = (jax.nn.silu(gate_part) * up_part).astype(jnp.bfloat16)
-    summed = lax.psum_scatter(
-        jnp.dot(units, draft_down, preferred_element_type=jnp.float32).astype(jnp.bfloat16),
-        RING,
-        scatter_dimension=0,
-        tiled=True,
-    ).astype(jnp.float32)
+    drafted = jnp.dot(units, draft_down, preferred_element_type=jnp.float32).astype(jnp.bfloat16)
+    summed = scatter(loop, 3, drafted.reshape(-1, rounds_total * requests_here, width))
     draft_out = rms_scale(features + summed, final_gain).astype(jnp.bfloat16)
     return (
         verified.reshape(hidden_rows.shape),
@@ -95,8 +339,9 @@
         P(("expert", "tensor"), None),
         P(),
     )
+    loop = Loop(dict(mesh.shape))
     return jax.shard_map(
-        local,
+        functools.partial(local, loop),
         mesh=mesh,
         in_specs=placed,
         out_specs=(

time: 301 us -> 170 us (0.56)
  waiting for transfers between devices: 200 us -> 0 us
  Pallas kernels: 0 us -> 106 us
  blocking collectives: 24 us -> 0 us
  between operations: 13.8 us -> 0.75 us
    reduce_scatter x2 -> x0, waiting for transfers between devices: 130 us -> none  [the longest x1 76.3 us: local(): mixed = lax.psum_scatter(part, RING, scatter_dimension=0, tiled=True)]
    pallas_call x0 -> x4, Pallas kernels: none -> 106 us  [the longest x2 53.5 us: scatter(): pl.pallas_call(functools.partial(scatter_kernel, loop), out_shape=jax.Sha...]
    all_gather x2 -> x0, waiting for transfers between devices: 69.5 us -> none  [the longest x1 36.9 us: local(): pieces = lax.all_gather(draft_input, RING, axis=0, tiled=True)]
    all_gather x1 -> x0, blocking collectives: 24 us -> none  [local(): table = lax.all_gather(table, RING, axis=0, tiled=True)]
  transfers between devices with their start and end apart: 4 -> 0, of which waited for: 4 -> 0; matrix products, arithmetic and copies ran while one was open for 2% -> 0% of each run, Pallas kernels for 0% -> 0%
where the time goes in v2:
time: 170 us; the launch traced here: 169 us
  Pallas kernels  106 us (62%)
  matrix products  37.8 us (22%)
  local copies, waits for them, and re-layouts  13.5 us (8%)
  other arithmetic  11.2 us (7%)
    pallas_call x2, Pallas kernels, scatter(): pl.pallas_call(functools.partial(scatter_kernel, loop), out_shape=jax.Sha...  53.5 us
    pallas_call x2, Pallas kernels, gather(): pl.pallas_call(functools.partial(gather_kernel, loop, pieces, len(arrays)...  52.5 us
    dot_general x1, matrix products, local(): part = jnp.dot(active, down_weight[0], preferred_element_type=jnp.float32)  18.5 us
    dot_general x1, matrix products, local(): jnp.dot(everyone, gate_weight[0], preferred_element_type=jnp.float32)  9.83 us
    dot_general x1, matrix products, local(): jnp.dot(units, draft_down, preferred_element_type=jnp.float32)  4.58 us
    convert_element_type x2, local copies, waits for them, and re-layouts, local(): rows = hidden_rows.reshape(total, width).astype(jnp.float32)  4.5 us
    unnamed x12, local copies, waits for them, and re-layouts  3.65 us
    dot_general x1, matrix products, local(): gate_part = jnp.dot(pieces, draft_gate, preferred_element_type=jnp.float32)  3.61 us

profile of v2, /device:TPU:0, one launch (start us, length us, event | category | flops | bytes accessed | tf_op | source)
XLA Modules:
  0.0 169.2 jit_solution(3346739377093732730)
XLA Ops:
  0.6 0.0 copy-start
  0.6 2.3 %copy.39 = f32[4,10,4096]{2,1,0:T(8,128)} copy(bf16[4,10,4096]{2,0,1:T(4,128)(2,1)} %param.13) | data formatting | bytes 983040 | tf_op jit(solution)/shard_map/convert_element_type | solution.py:282
  3.0 2.2 %reshape.97 = f32[40,4096]{1,0:T(8,128)} reshape(f32[4,10,4096]{2,1,0:T(8,128)} %copy.39) | data formatting | bytes 1310720 | tf_op jit(solution)/shard_map/convert_element_type | solution.py:282
  5.1 1.2 multiply_reduce_fusion
  6.4 0.1 copy.47
  6.5 0.1 rsqrt.31
  6.6 1.2 multiply_convert_fusion.2.refs_0_
  7.8 0.0 copy-start.2
  7.8 0.7 copy.41
  8.6 0.1 eq.40
  8.7 0.1 copy.43
  8.8 1.2 fusion.27
  10.0 0.1 broadcast_divide_fusion
  10.1 0.6 pad.4.refs_1_
  10.7 0.0 copy-done.2
  10.7 35.8 %shard_map.140 = (bf16[16,40,4096]{2,1,0:T(8,128)(2,1)}, f32[16,40,128]{2,1,0:T(8,128)}) custom-call(bf16[40,4096]{1,0:T(8,128)(2,1)} %copy-done.2, f32[40,128]{1,0:T(8,128)} %pad.4.refs_1_), custom_call_target="tpu_custom_call" | custom-call | tf_op jit(solution)/shard_map/pallas_call | solution.py:139
  46.5 1.1 select_reduce_fusion.1
  47.7 0.1 mul.92
  47.8 9.8 %fusion.3 = f32[640,768]{1,0:T(8,128)} fusion(bf16[640,4096]{1,0:T(8,128)(2,1)} %bitcast.34, bf16[1,4096,768]{2,1,0:T(8,128)(2,1)} %param.18), kind=kOutput, calls=%fused_computation.4 | convolution fusion | flops 4026531840 | bytes 13500416 | tf_op jit(solution)/shard_map/dot_general | solution.py:299
  57.6 18.5 %multiply_convert_fusion = bf16[640,4096]{1,0:T(8,128)(2,1)} fusion(bf16[1,768,4096]{2,1,0:T(8,128)(2,1)} %param.20, f32[640]{0:T(1024)S(1)} %mul.92, f32[640,768]{1,0:T(8,128)} %fusion.3, bf16[640,4096]{1,0:T(8,128)(2,1)} %bitcast.35, bf16[1,4096,768]{2,1,0:T(8,128)(2,1)} %param.19), kind=kOutput, calls=%fused_computation | convolution fusion | flops 8061255680 | bytes 25037312 | tf_op jit(solution)/shard_map/dot_general | solution.py:302
  76.1 0.0 copy-start.1
  76.1 36.2 %shard_map.141 = f32[40,4096]{1,0:T(8,128)} custom-call(bf16[16,40,4096]{2,1,0:T(8,128)(2,1)} %bitcast.33), custom_call_target="tpu_custom_call" | custom-call | tf_op jit(solution)/shard_map/pallas_call | solution.py:241
  112.3 0.0 copy-done.1
  112.3 1.1 add_convert_fusion
  113.4 1.1 reshape.98
  114.5 0.8 copy.44
  115.3 0.1 iota_compare_fusion.1
  115.4 2.4 %select_reduce_fusion = f32[4,2,4096]{2,1,0:T(2,128)} fusion(f32[4,2,5,4096]{3,2,1,0:T(8,128)} %reshape.98, pred[4,2,5]{2,1,0:T(4,128)(4,1)S(1)} %iota_compare_fusion.1), kind=kLoop, calls=%fused_computation.16 | loop fusion | flops 294912 | bytes 786472 | tf_op jit(solution)/shard_map/reduce_sum | solution.py:309
  117.7 1.6 reshape.93
  119.4 1.1 multiply_reduce_fusion.2
  120.4 0.1 rsqrt.33
  120.5 1.6 multiply_convert_fusion.4.refs_0_
  122.2 16.7 %shard_map.142 = bf16[16,8,4096]{2,1,0:T(8,128)(2,1)} custom-call(bf16[8,4096]{1,0:T(8,128)(2,1)} %multiply_convert_fusion.4.refs_0_), custom_call_target="tpu_custom_call" | custom-call | tf_op jit(solution)/shard_map/pallas_call | solution.py:139
  138.8 3.6 %fusion.13 = f32[128,384]{1,0:T(8,128)} fusion(bf16[4096,384]{1,0:T(8,128)(2,1)} %param.22, bf16[16,8,4096]{2,1,0:T(8,128)(2,1)} %shard_map.142), kind=kOutput, calls=%fused_computation.14 | convolution fusion | flops 402653184 | bytes 4390912 | tf_op jit(solution)/shard_map/dot_general | solution.py:314
  142.4 0.0 copy-done
  142.4 0.0 copy-start.3
  142.4 4.6 %fusion.5.part = bf16[16,8,4096]{2,1,0:T(8,128)(2,1)} fusion(bf16[384,4096]{1,0:T(8,128)(2,1)S(1)} %copy-done, bf16[4096,384]{1,0:T(8,128)(2,1)} %param.23, bf16[16,8,4096]{2,1,0:T(8,128)(2,1)} %shard_map.142, f32[128,384]{1,0:T(8,128)} %fusion.13), kind=kOutput, calls=%fused_computation.7 | convolution fusion | flops 806125568 | bytes 8585216 | tf_op jit(solution)/shard_map/dot_general | solution.py:317
  147.0 17.3 %shard_map.143 = f32[8,4096]{1,0:T(8,128)} custom-call(bf16[16,8,4096]{2,1,0:T(8,128)(2,1)} %fusion.5.part), custom_call_target="tpu_custom_call" | custom-call | tf_op jit(solution)/shard_map/pallas_call | solution.py:241
  164.3 1.1 multiply_reduce_fusion.1
  165.5 0.0 copy-done.3
  165.5 0.1 multiply_convert_fusion.3
  165.6 0.7 reshape.96
  166.2 0.9 reshape.92
  167.1 2.0 %copy.45 = bf16[4,10,4096]{2,0,1:T(4,128)(2,1)} copy(bf16[4,10,4096]{2,1,0:T(8,128)(2,1)} %reshape.92) | data formatting | bytes 655360
  (5 shorter events, 0.1 us)
Async XLA Ops:
  0.6 141.8 %copy-start = (bf16[384,4096]{1,0:T(8,128)(2,1)S(1)}, bf16[384,4096]{1,0:T(8,128)(2,1)}, u32[]{:S(2)}) copy-start(bf16[384,4096]{1,0:T(8,128)(2,1)} %param.24) | copy-start | bytes 9437188
  7.8 2.9 %copy-start.2 = (bf16[40,4096]{1,0:T(8,128)(2,1)}, bf16[40,4096]{1,0:T(8,128)(2,1)S(1)}, u32[]{:S(2)}) copy-start(bf16[40,4096]{1,0:T(8,128)(2,1)S(1)} %multiply_convert_fusion.2.refs_0_) | copy-start | bytes 983044
  76.1 36.2 %copy-start.1 = (f32[40,4096]{1,0:T(8,128)S(1)}, f32[40,4096]{1,0:T(8,128)}, u32[]{:S(2)}) copy-start(f32[40,4096]{1,0:T(8,128)} %reshape.97) | copy-start | bytes 1966084
  142.4 23.0 %copy-start.3 = (f32[4096]{0:T(1024)S(1)}, f32[4096]{0:T(1024)}, u32[]{:S(2)}) copy-start(f32[4096]{0:T(1024)} %param.25) | copy-start | bytes 49156

commit v3 on v2

--- a/solution.py
+++ b/solution.py
@@ -256,6 +256,292 @@
     return values * lax.rsqrt(mean_square + EPSILON) * weights
 
 
+def fused_kernel(loop, gated, pieces, batches, *refs):
+    inputs = 2 if gated else 1
+    sources = refs[:inputs]
+    weights = refs[inputs : inputs + 3]
+    out = refs[inputs + 3]
+    rest = refs[inputs + 4 :]
+    held, rest = rest[:inputs], rest[inputs:]
+    gate_w, up_w, down_w, rows_all, active, part, stage, arrived = rest[:8]
+    ring_send, ring_recv, sum_send, sum_recv, weight_sem, own_sem = rest[8:14]
+    p, lane = loop.me()
+    n, last, lanes = loop.n, loop.half, loop.lanes
+    if lanes == 2:
+        from_pair, pair_send, pair_recv, back_send, back_recv = rest[14:]
+    count = len(pieces)
+    rows, width = sources[0].shape
+    columns = width // 2
+    hidden = gate_w.shape[1]
+
+    loads = []
+    for i, (ref, buffer) in enumerate(zip(weights, (gate_w, up_w, down_w))):
+        loads.append(pltpu.make_async_copy(ref, buffer, weight_sem.at[i]))
+        loads[-1].start()
+    loop.greet(p, lane)
+
+    def slot(way, step, other):
+        if step == 0:
+            return other
+        if step == last:
+            return lanes * (2 * last - 1) + other
+        return lanes * (2 * step - 1 + way) + other
+
+    def source(c):
+        which, start, size = pieces[c]
+        return sources[which].at[:, pl.ds(start, size)]
+
+    def landed(index, c):
+        which, start, size = pieces[c]
+        return held[which].at[index, :, pl.ds(start, size)]
+
+    def used(way, step, c):
+        return step < last or c % 2 == way
+
+    ring, pair, waited = {}, {}, set()
+
+    def send(way, step, c):
+        ring[way, step, c] = pltpu.make_async_remote_copy(
+            src_ref=source(c) if step == 1 else landed(slot(way, step - 1, 0), c),
+            dst_ref=landed(slot(way, step, 0), c),
+            send_sem=ring_send.at[way, step - 1, c],
+            recv_sem=ring_recv.at[way, step - 1, c],
+            device_id=loop.device(p + 1 if way == 0 else p - 1, lane),
+            device_id_type=MESH,
+        )
+        ring[way, step, c].start()
+
+    def share(way, step, c):
+        if lanes == 1:
+            return
+        k = way * last + step
+        pair[slot(way, step, 1), c] = pltpu.make_async_remote_copy(
+            src_ref=source(c) if step == 0 else landed(slot(way, step, 0), c),
+            dst_ref=landed(slot(way, step, 1), c),
+            send_sem=pair_send.at[k, c],
+            recv_sem=pair_recv.at[k, c],
+            device_id=loop.device(p, 1 - lane),
+            device_id_type=MESH,
+        )
+        pair[slot(way, step, 1), c].start()
+
+    for c in range(count):
+        for way in range(2):
+            if used(way, 1, c):
+                send(way, 1, c)
+    keep = []
+    for c in range(count):
+        share(0, 0, c)
+        keep.append(pltpu.make_async_copy(source(c), landed(0, c), own_sem.at[c]))
+        keep[-1].start()
+
+    def receive(step, wanted):
+        for c in wanted:
+            for way in range(2):
+                if used(way, step, c):
+                    ring[way, step, c].wait_recv()
+                    if step < last and used(way, step + 1, c):
+                        send(way, step + 1, c)
+                    share(way, step, c)
+
+    sums = {}
+
+    def returned(offset):
+        far, way = (offset, 1) if offset <= last else (n - offset, 0)
+        return slot(way, far, 0)
+
+    def send_back(first, stop):
+        if lanes == 1:
+            return
+        for far in range(last, -1, -1):
+            for offset in sorted({far, (n - far) % n}):
+                at = returned(offset)
+                if first <= at < stop:
+                    sums[offset] = pltpu.make_async_remote_copy(
+                        src_ref=part.at[at + 1],
+                        dst_ref=from_pair.at[offset],
+                        send_sem=back_send.at[offset],
+                        recv_sem=back_recv.at[offset],
+                        device_id=loop.device(p, 1 - lane),
+                        device_id_type=MESH,
+                    )
+                    sums[offset].start()
+
+    def compute(batch, between):
+        first, stop = batch
+        size = (stop - first) * rows
+        for (index, c), copy in pair.items():
+            if first <= index < stop and (index, c) not in waited:
+                waited.add((index, c))
+                copy.wait_recv()
+        tile = 512
+
+        def take(i, carry):
+            span = pl.ds(pl.multiple_of(i * tile, tile), tile)
+            block = held[0][pl.ds(first, stop - first), :, span].astype(jnp.float32)
+            rows_all[pl.ds(0, size), span] = block.reshape(size, tile).astype(jnp.bfloat16)
+            return carry
+
+        lax.fori_loop(0, width // tile, take, 0)
+        wide = 256 if hidden % 256 == 0 else 128
+
+        def units(i, carry):
+            span = pl.ds(pl.multiple_of(i * wide, wide), wide)
+            x = rows_all[pl.ds(0, size), :]
+            gate = jnp.dot(x, gate_w[:, span], preferred_element_type=jnp.float32)
+            up = jnp.dot(x, up_w[:, span], preferred_element_type=jnp.float32)
+            value = gate / (1.0 + jnp.exp(-gate)) * up
+            active[pl.ds(0, size), span] = value.astype(jnp.bfloat16)
+            return carry
+
+        lax.fori_loop(0, hidden // wide, units, 0)
+        between()
+        if gated:
+            mine = lax.axis_index("expert") * loop.tensor + lax.axis_index("tensor")
+            table = held[1][pl.ds(first, stop - first), :, :]
+            table = table.reshape(size, table.shape[2])
+            here = lax.broadcasted_iota(jnp.int32, table.shape, 1) == mine
+            weight = jnp.sum(jnp.where(here, table, 0.0), axis=1, keepdims=True)
+
+        def down(i, carry):
+            span = pl.ds(pl.multiple_of(i * tile, tile), tile)
+            value = jnp.dot(
+                active[pl.ds(0, size), :], down_w[:, span], preferred_element_type=jnp.float32
+            )
+            if gated:
+                value = value * weight
+            part[pl.ds(first, stop - first), :, span] = value.reshape(
+                stop - first, rows, tile
+            ).astype(jnp.bfloat16)
+            return carry
+
+        lax.fori_loop(0, width // tile, down, 0)
+        send_back(first, stop)
+
+    for copy in keep:
+        copy.wait()
+    ready = False
+    for step in range(1, last + 1):
+        done = batches.get(step - 1)
+        if done is None:
+            receive(step, range(count))
+            continue
+        if not ready:
+            ready = True
+            for copy in loads:
+                copy.wait()
+        compute(done, lambda: receive(step, range(1)))
+        receive(step, range(1, count))
+    if not ready:
+        for copy in loads:
+            copy.wait()
+    compute(batches[last], lambda: None)
+
+    seen = set()
+
+    def mine_of(offset, h):
+        span = pl.ds(h * columns, columns)
+        value = part[returned(offset), :, span].astype(jnp.float32)
+        if lanes == 2:
+            if offset not in seen:
+                seen.add(offset)
+                sums[offset].wait_recv()
+            value = value + from_pair[offset, :, span].astype(jnp.float32)
+        return value
+
+    def moves(way, step, h):
+        return 1 <= step <= last and (way == h or step >= 2)
+
+    back = {}
+    for step in range(1, last + 1):
+        for h in range(2):
+            for way in range(2):
+                if not moves(way, step, h):
+                    continue
+                far = last + 1 - step
+                value = mine_of(far if way == 0 else (n - far) % n, h)
+                if moves(way, step - 1, h):
+                    back[way, step - 1, h].wait_recv()
+                    value = value + arrived[way, step - 2, h].astype(jnp.float32)
+                stage[way, step - 1, h] = value.astype(jnp.bfloat16)
+                back[way, step, h] = pltpu.make_async_remote_copy(
+                    src_ref=stage.at[way, step - 1, h],
+                    dst_ref=arrived.at[way, step - 1, h],
+                    send_sem=sum_send.at[way, step - 1, h],
+                    recv_sem=sum_recv.at[way, step - 1, h],
+                    device_id=loop.device(p + 1 if way == 0 else p - 1, lane),
+                    device_id_type=MESH,
+                )
+                back[way, step, h].start()
+    for h in range(2):
+        value = mine_of(0, h)
+        for way in range(2):
+            if moves(way, last, h):
+                back[way, last, h].wait_recv()
+                value = value + arrived[way, last - 1, h].astype(jnp.float32)
+        out[:, pl.ds(h * columns, columns)] = value
+    for group in (ring, pair, sums, back):
+        for copy in group.values():
+            copy.wait_send()
+
+
+def cut(arrays):
+    pieces = []
+    for which, array in enumerate(arrays):
+        width = array.shape[1]
+        cuts = 2 if width >= 1024 else 1
+        for i in range(cuts):
+            pieces.append((which, i * width // cuts, width // cuts))
+    return pieces
+
+
+def fused(loop, collective_id, early, arrays, weights):
+    rows, width = arrays[0].shape
+    hidden = weights[0].shape[1]
+    n, last, lanes = loop.n, loop.half, loop.lanes
+    pieces = cut(arrays)
+    count = len(pieces)
+    blocks = n * lanes
+    if early and last >= 3:
+        batches = {1: (0, 3 * lanes)}
+        for step in range(2, last):
+            batches[step] = (lanes * (2 * step - 1), lanes * (2 * step + 1))
+        batches[last] = (lanes * (2 * last - 1), blocks)
+    else:
+        batches = {last: (0, blocks)}
+    most = max(stop - first for first, stop in batches.values()) * rows
+    dma, half = pltpu.SemaphoreType.DMA, jnp.bfloat16
+    scratch = [pltpu.VMEM((blocks,) + a.shape, a.dtype) for a in arrays]
+    scratch += [pltpu.VMEM(w.shape, w.dtype) for w in weights]
+    scratch += [
+        pltpu.VMEM((most, width), half),
+        pltpu.VMEM((most, hidden), half),
+        pltpu.VMEM((blocks, rows, width), half),
+        pltpu.VMEM((2, last, 2, rows, width // 2), half),
+        pltpu.VMEM((2, last, 2, rows, width // 2), half),
+    ]
+    need = sum(2 * (-(-rows // 16) * 16) * width * k for k in (2 * blocks, 4 * last, n))
+    need += sum(w.size * 2 for w in weights) + 2 * most * (width + hidden) + 2**23
+    if need > 58 * 2**20:
+        return None
+    scratch += [dma((2, last, count)), dma((2, last, count)), dma((2, last, 2)), dma((2, last, 2))]
+    scratch += [dma((3,)), dma((count,))]
+    if lanes == 2:
+        scratch += [pltpu.VMEM((n, rows, width), half)]
+        scratch += [dma((2 * last + 1, count)), dma((2 * last + 1, count)), dma((n,)), dma((n,))]
+    memory = [pltpu.VMEM] * len(arrays) + [pl.ANY] * 3
+    return pl.pallas_call(
+        functools.partial(fused_kernel, loop, len(arrays) == 2, pieces, batches),
+        out_shape=jax.ShapeDtypeStruct((rows, width), jnp.float32),
+        in_specs=[pl.BlockSpec(memory_space=space) for space in memory],
+        out_specs=pl.BlockSpec(memory_space=pltpu.VMEM),
+        scratch_shapes=scratch,
+        compiler_params=pltpu.CompilerParams(
+            collective_id=collective_id, has_side_effects=True, vmem_limit_bytes=60 * 2**20
+        ),
+    )(*arrays, *weights)
+
+
 def local(
     loop,
     hidden_rows,
@@ -289,19 +575,24 @@
 
     lanes_wide = -(-expert_count // 128) * 128
     table = jnp.pad(table, ((0, 0), (0, lanes_wide - expert_count)))
-    everyone, tables = gather(loop, 0, normed, table)
-    everyone = everyone.reshape(-1, width)
-    share = jnp.sum(
-        jnp.where(jnp.arange(lanes_wide) == my_expert, tables.reshape(-1, lanes_wide), 0.0),
-        axis=1,
-        keepdims=True,
+    mixed = fused(
+        loop, 0, True, (normed, table), (gate_weight[0], up_weight[0], down_weight[0])
     )
-    gate_values = jnp.dot(everyone, gate_weight[0], preferred_element_type=jnp.float32)
-    up_values = jnp.dot(everyone, up_weight[0], preferred_element_type=jnp.float32)
-    active = (jax.nn.silu(gate_values) * up_values).astype(jnp.bfloat16)
-    part = jnp.dot(active, down_weight[0], preferred_element_type=jnp.float32)
-    part = (share * part).astype(jnp.bfloat16)
-    mixed = lax.psum(scatter(loop, 1, part.reshape(-1, total, width)), "sub")
+    if mixed is None:
+        everyone, tables = gather(loop, 0, normed, table)
+        everyone = everyone.reshape(-1, width)
+        share = jnp.sum(
+            jnp.where(jnp.arange(lanes_wide) == my_expert, tables.reshape(-1, lanes_wide), 0.0),
+            axis=1,
+            keepdims=True,
+        )
+        gate_values = jnp.dot(everyone, gate_weight[0], preferred_element_type=jnp.float32)
+        up_values = jnp.dot(everyone, up_weight[0], preferred_element_type=jnp.float32)
+        active = (jax.nn.silu(gate_values) * up_values).astype(jnp.bfloat16)
+        part = jnp.dot(active, down_weight[0], preferred_element_type=jnp.float32)
+        part = (share * part).astype(jnp.bfloat16)
+        mixed = scatter(loop, 1, part.reshape(-1, total, width))
+    mixed = lax.psum(mixed, "sub")
     verified = (rows + mixed).astype(jnp.bfloat16)
 
     by_request = verified.reshape(rounds_total, requests_here, draft_rows, width)
@@ -309,13 +600,15 @@
     features = jnp.sum(jnp.where(pick[..., None], by_request.astype(jnp.float32), 0.0), axis=2)
     features = features.reshape(rounds_total * requests_here, width)
     draft_input = rms_scale(features, draft_gain).astype(jnp.bfloat16)
-    (pieces,) = gather(loop, 2, draft_input)
-    pieces = pieces.reshape(-1, width)
-    gate_part = jnp.dot(pieces, draft_gate, preferred_element_type=jnp.float32)
-    up_part = jnp.dot(pieces, draft_up, preferred_element_type=jnp.float32)
-    units = (jax.nn.silu(gate_part) * up_part).astype(jnp.bfloat16)
-    drafted = jnp.dot(units, draft_down, preferred_element_type=jnp.float32).astype(jnp.bfloat16)
-    summed = scatter(loop, 3, drafted.reshape(-1, rounds_total * requests_here, width))
+    summed = fused(loop, 2, False, (draft_input,), (draft_gate, draft_up, draft_down))
+    if summed is None:
+        (pieces,) = gather(loop, 2, draft_input)
+        pieces = pieces.reshape(-1, width)
+        gate_part = jnp.dot(pieces, draft_gate, preferred_element_type=jnp.float32)
+        up_part = jnp.dot(pieces, draft_up, preferred_element_type=jnp.float32)
+        units = (jax.nn.silu(gate_part) * up_part).astype(jnp.bfloat16)
+        drafted = jnp.dot(units, draft_down, preferred_element_type=jnp.float32).astype(jnp.bfloat16)
+        summed = scatter(loop, 3, drafted.reshape(-1, rounds_total * requests_here, width))
     draft_out = rms_scale(features + summed, final_gain).astype(jnp.bfloat16)
     return (
         verified.reshape(hidden_rows.shape),

time: 170 us -> 125 us (0.74)
  matrix products: 37.8 us -> 0.34 us
  local copies, waits for them, and re-layouts: 13.5 us -> 5.22 us
  Pallas kernels: 106 us -> 112 us
  other arithmetic: 11.2 us -> 5.9 us
    dot_general x4 -> x0, matrix products: 36.5 us -> none  [the longest x1 18.5 us: local(): part = jnp.dot(active, down_weight[0], preferred_element_type=jnp.float32)]
    pallas_call x4 -> x2, Pallas kernels: 106 us -> 112 us  [fused(): pl.pallas_call(functools.partial(fused_kernel, loop, len(arrays) == 2, pi...]
    convert_element_type x2, local copies, waits for them, and re-layouts: 4.5 us -> 1.31 us  [local(): rows = hidden_rows.reshape(total, width).astype(jnp.float32)]
    reduce_sum x1, other arithmetic: 2.37 us -> 0.45 us  [local(): jnp.sum(jnp.where(pick[..., None], by_request.astype(jnp.float32), 0.0),...]
    unnamed x12 -> x14, local copies, waits for them, and re-layouts: 3.65 us -> 1.94 us
where the time goes in v3:
time: 125 us; the launch traced here: 124 us
  Pallas kernels  112 us (90%)
  other arithmetic  5.9 us (5%)
  local copies, waits for them, and re-layouts  5.22 us (4%)
    pallas_call x2, Pallas kernels, fused(): pl.pallas_call(functools.partial(fused_kernel, loop, len(arrays) == 2, pi...  112 us

profile of v3, /device:TPU:0, one launch (start us, length us, event | category | flops | bytes accessed | tf_op | source)
XLA Modules:
  0.0 124.5 jit_solution(4332229834507916903)
XLA Ops:
  0.6 0.0 copy-start
  0.6 1.2 copy.39
  1.9 0.1 reshape.73
  2.0 1.2 multiply_reduce_fusion
  3.2 0.1 copy.47
  3.3 0.1 rsqrt.31
  3.4 0.8 multiply_convert_fusion.refs_0_
  4.2 0.0 copy-start.1
  4.3 0.7 copy.41
  5.0 0.1 eq.32
  5.1 0.1 copy.43
  5.2 0.0 copy-done
  5.2 0.3 fusion.2
  5.5 0.1 broadcast_divide_fusion
  5.6 0.6 pad.4.refs_1_
  6.3 0.0 copy-done.1
  6.3 0.0 copy-start.4
  6.3 0.0 copy-start.2
  6.3 78.2 %shard_map.140 = f32[40,4096]{1,0:T(8,128)} custom-call(bf16[40,4096]{1,0:T(8,128)(2,1)} %copy-done.1, f32[40,128]{1,0:T(8,128)} %pad.4.refs_1_, bf16[4096,768]{1,0:T(8,128)(2,1)} %bitcast.7, bf16[4096,768]{1,0:T(8,128)(2,1)} %bitcast.8, bf16[768,4096]{1,0:T(8,128)(2,1)} %bitcast.9), custom_call_target="tpu_custom_call" | custom-call | tf_op jit(solution)/shard_map/pallas_call | solution.py:533
  84.4 1.1 add_convert_fusion
  85.6 0.0 copy-start.3
  85.6 0.1 reshape.74
  85.7 0.0 copy-done.4
  85.7 0.1 copy.44
  85.8 0.1 iota_compare_fusion.1
  85.9 0.5 select_reduce_fusion
  86.3 0.1 reshape.71
  86.4 0.1 multiply_reduce_fusion.2
  86.6 0.1 rsqrt.33
  86.7 0.0 copy-done.2
  86.7 0.7 multiply_convert_fusion.2.refs_0_
  87.4 34.1 %shard_map.141 = f32[8,4096]{1,0:T(8,128)} custom-call(bf16[8,4096]{1,0:T(8,128)(2,1)} %multiply_convert_fusion.2.refs_0_, bf16[4096,384]{1,0:T(8,128)(2,1)} %refs_1_.1, bf16[4096,384]{1,0:T(8,128)(2,1)} %refs_2_.1, bf16[384,4096]{1,0:T(8,128)(2,1)} %refs_3_.1), custom_call_target="tpu_custom_call" | custom-call | tf_op jit(solution)/shard_map/pallas_call | solution.py:533
  121.6 1.1 multiply_reduce_fusion.1
  122.6 0.0 copy-done.3
  122.6 0.1 multiply_convert_fusion.1
  122.7 0.7 reshape.72
  123.4 0.1 reshape.70
  123.5 1.0 copy.45
  (4 shorter events, 0.0 us)
Async XLA Ops:
  0.6 4.6 %copy-start = (bf16[4096,16]{0,1:T(8,128)(2,1)S(1)}, bf16[4096,16]{0,1:T(8,128)(2,1)}, u32[]{:S(2)}) copy-start(bf16[4096,16]{0,1:T(8,128)(2,1)} %param.17) | copy-start | bytes 393220
  4.2 2.0 %copy-start.1 = (bf16[40,4096]{1,0:T(8,128)(2,1)}, bf16[40,4096]{1,0:T(8,128)(2,1)S(1)}, u32[]{:S(2)}) copy-start(bf16[40,4096]{1,0:T(8,128)(2,1)S(1)} %multiply_convert_fusion.refs_0_) | copy-start | bytes 983044
  6.3 79.4 %copy-start.4 = (s32[4,2]{0,1:T(2,128)S(1)}, s32[4,2]{0,1:T(2,128)}, u32[]{:S(2)}) copy-start(s32[4,2]{0,1:T(2,128)} %param.15) | copy-start | bytes 100
  6.3 80.4 %copy-start.2 = (f32[4096]{0:T(1024)S(1)}, f32[4096]{0:T(1024)}, u32[]{:S(2)}) copy-start(f32[4096]{0:T(1024)} %param.21) | copy-start | bytes 49156
  85.6 37.0 %copy-start.3 = (f32[4096]{0:T(1024)S(1)}, f32[4096]{0:T(1024)}, u32[]{:S(2)}) copy-start(f32[4096]{0:T(1024)} %param.25) | copy-start | bytes 49156
